TPU v7x, 256 devices: a whole 4x4x8 slice. The times are simulated.
256 devices in a mesh: ctx: 16 (over z_hi, y, core), exp: 16 (over z_lo, x).
Axes of the slice: x: 4, y: 4, z: 8 (z_hi: 2, z_lo: 4; z = z_hi * 4 + z_lo), core: 2. Of those that a mesh axis runs over, the one named last changes fastest.
Arguments:
- residual: bfloat16 [16, 2048, 7168], P('exp', 'ctx'), may hold values from -6 to 6
- queries: bfloat16 [16, 2048, 1024], P('exp', 'ctx'), may hold values from -64 to 64
- latent: bfloat16 [16, 2048, 512], P('exp', 'ctx'), may hold values from -6 to 6
- out_proj: bfloat16 [1024, 7168], P('ctx'), may hold values from -0.5 to 0.5
- up_weight: bfloat16 [16, 7168, 1024], P('exp', 'ctx'), may hold values from -0.0625 to 0.0625
- down_weight: bfloat16 [16, 1024, 7168], P('exp', None, 'ctx'), may hold values from -0.1875 to 0.1875
- cotangent: bfloat16 [16, 2048, 7168], P('exp', 'ctx'), may hold values from -6 to 6
- routes: int32 [16, 2048, 8], P('exp', 'ctx'), may hold values from 0 to 255, as said below
- gate_values: float32 [16, 2048, 8], P('exp', 'ctx'), may hold values from 0.2 to 1
- documents: int32 [16, 16], P('exp'), may hold values from 0 to 2, never falling along the last dimension, each value on 1 to 8 neighbouring positions
Outputs:
- layer_out: bfloat16 [16, 2048, 7168], P('exp', 'ctx')
- input_grad: bfloat16 [16, 2048, 7168], P('exp', 'ctx')
- up_grad: bfloat16 [16, 7168, 1024], P('exp', 'ctx')
- down_grad: bfloat16 [16, 1024, 7168], P('exp', None, 'ctx')
Inputs may be any that keep to these rules, and one draw needn't show every extreme that they name: Each token's 8 experts differ. Within one block of 128 consecutive tokens of a sequence at most 4 routes name one expert below 16, and in every draw some expert below 16 is named by exactly 4 routes of every such block. `documents`: document numbers never fall along a sequence; a document covers 1 to 8 consecutive blocks, and one covers exactly 8.
All inputs are finite; a program needn't handle non-finite values.
Results may differ from a plain program's by a relative error of at most 0.025.
Values may be sent and summed in bfloat16 or wider, within the bound.
No kernel may reach another device: no remote copies, remote signals or barrier semaphores. Data moves between devices by JAX's collectives and lax.ppermute only.
A program may use at most 128 MiB of HBM per device.

v0:
```python
import math
import jax
import jax.numpy as jnp
from jax import lax
from jax.sharding import PartitionSpec as P

LAT = 512
HEADS = 2
CAP = 4
BLOCK = 128


def shifted(shard, axis, by):
    peers = lax.axis_size(axis)
    pairs = [(i, i + by) for i in range(peers) if 0 <= i + by < peers]
    return lax.ppermute(shard, axis, pairs)


def split_up(shard, dim, peers):
    dims = shard.shape
    pieces = shard.reshape(*dims[:dim], peers, dims[dim] // peers, *dims[dim + 1 :])
    return jnp.moveaxis(pieces, dim, 0)


def laid_out(pieces, dim):
    pieces = jnp.moveaxis(pieces, 0, dim)
    dims = pieces.shape
    return pieces.reshape(*dims[:dim], dims[dim] * dims[dim + 1], *dims[dim + 2 :])


def joined_exchange(shard, axis, axes, splits, concats):
    sizes = [lax.axis_size(a) for a in axes]
    pieces = split_up(shard, splits[0], sizes[0])
    pieces = jnp.moveaxis(split_up(pieces, splits[1] + 1, sizes[1]), 0, 1)
    inside = pieces.shape[2:]
    pieces = pieces.reshape(-1, *inside)
    pieces = lax.all_to_all(pieces, axis, split_axis=0, concat_axis=0, tiled=True)
    pieces = laid_out(pieces.reshape(*sizes, *inside), concats[0] + 1)
    return laid_out(pieces, concats[1])


def silu_grad(values_in):
    sigmoid_of = jax.nn.sigmoid(values_in)
    return sigmoid_of * (1.0 + values_in * (1.0 - sigmoid_of))


def slot_tables(route_rows, gate_rows, expert_total, capacity):
    experts = jnp.arange(expert_total, dtype=jnp.int32)
    onehot = (route_rows[:, :, None] == experts[None, None, :]).astype(jnp.int32)
    flat_hits = onehot.reshape(-1, expert_total)
    before = jnp.cumsum(flat_hits, axis=0) - flat_hits
    rank_in = jnp.sum(before * flat_hits, axis=1).reshape(route_rows.shape)
    valid = route_rows < expert_total
    slot_index = jnp.where(valid, route_rows * capacity + rank_in, -1)
    slots_all = jnp.arange(expert_total * capacity, dtype=jnp.int32)
    slot_hits = slot_index[None, :, :] == slots_all[:, None, None]
    picker = jnp.sum(slot_hits.astype(jnp.float32), axis=2)
    weigher = jnp.sum(jnp.where(slot_hits, gate_rows[None, :, :], 0.0), axis=2)
    return (picker, weigher)


def shards(
    residual,
    queries,
    latent,
    out_proj,
    up_weight,
    down_weight,
    cotangent,
    routes,
    gate_values,
    documents,
):
    ctx_count = lax.axis_size("ctx")
    exp_count = lax.axis_size("exp")
    my_index = lax.axis_index("ctx")
    tokens = residual.shape[1]
    model_width = residual.shape[2]
    doc_row = documents[0]
    block_total = doc_row.shape[0]
    inv_root = 1.0 / math.sqrt(LAT)
    query_rows = queries[0].reshape(tokens, HEADS, LAT)
    token_iota = jnp.arange(tokens, dtype=jnp.int32)
    block_iota = jnp.arange(block_total, dtype=jnp.int32)

    def doc_of(positions):
        matches = (positions // BLOCK)[:, None] == block_iota[None, :]
        return jnp.sum(jnp.where(matches, doc_row[None, :], 0), axis=1)

    query_pos = my_index * tokens + token_iota
    query_doc = doc_of(query_pos)

    def fold_keys(running_max, running_sum, weighted, key_block, source):
        key_pos = source * tokens + token_iota
        allowed = (
            (query_doc[:, None] == doc_of(key_pos)[None, :])
            & (key_pos[None, :] <= query_pos[:, None])
            & (source >= 0)
        )
        scores = (
            jnp.einsum("thk,jk->thj", query_rows, key_block, preferred_element_type=jnp.float32)
            * inv_root
        )
        scores = jnp.where(allowed[:, None, :], scores, -1e30)
        new_max = jnp.maximum(running_max, jnp.max(scores, axis=2))
        exponent = jnp.where(allowed[:, None, :], jnp.exp(scores - new_max[:, :, None]), 0.0)
        rescale = jnp.exp(running_max - new_max)
        running_sum = running_sum * rescale + jnp.sum(exponent, axis=2)
        weighted = weighted * rescale[:, :, None] + jnp.einsum(
            "thj,jk->thk",
            exponent.astype(jnp.bfloat16),
            key_block,
            preferred_element_type=jnp.float32,
        )
        return (new_max, running_sum, weighted)

    start_max = jnp.full((tokens, HEADS), -1e30, jnp.float32)
    start_sum = jnp.zeros((tokens, HEADS), jnp.float32)
    start_acc = jnp.zeros((tokens, HEADS, LAT), jnp.float32)
    first_max, first_sum, first_acc = fold_keys(
        start_max, start_sum, start_acc, latent[0], my_index
    )
    cycle_turns = ctx_count - 1

    def cycle_turn(cycle_step, loop_carry):
        key_block, running_max, running_sum, weighted = loop_carry
        key_block = shifted(key_block, "ctx", 1)
        running_max, running_sum, weighted = fold_keys(
            running_max, running_sum, weighted, key_block, my_index - cycle_step
        )
        return (key_block, running_max, running_sum, weighted)

    loop_carry = lax.fori_loop(
        1, cycle_turns + 1, cycle_turn, (latent[0], first_max, first_sum, first_acc)
    )
    heads_out = (
        (loop_carry[3] / loop_carry[2][:, :, None])
        .astype(jnp.bfloat16)
        .reshape(tokens, HEADS * LAT)
    )
    projected = jnp.dot(
        heads_out,
        lax.all_gather(out_proj, "ctx", axis=0, tiled=True),
        preferred_element_type=jnp.float32,
    )
    hidden_in = (residual[0].astype(jnp.float32) + projected).astype(jnp.bfloat16)
    picker, weigher = slot_tables(routes[0], gate_values[0], exp_count, CAP)
    picker_half = picker.astype(jnp.bfloat16)
    slot_gate = jnp.sum(weigher, axis=1)
    slot_in = jnp.dot(picker_half, hidden_in, preferred_element_type=jnp.float32).astype(
        jnp.bfloat16
    )
    slot_cot = (
        jnp.dot(picker_half, cotangent[0], preferred_element_type=jnp.float32) * slot_gate[:, None]
    ).astype(jnp.bfloat16)
    slot_in = slot_in.reshape(1, exp_count, CAP, model_width)
    slot_cot = slot_cot.reshape(1, exp_count, CAP, model_width)
    arrived_in, arrived_cot = (
        joined_exchange(slot_in, ("ctx", "exp"), ("ctx", "exp"), (3, 1), (0, 1)),
        joined_exchange(slot_cot, ("ctx", "exp"), ("ctx", "exp"), (3, 1), (0, 1)),
    )
    part_width = model_width // ctx_count
    row_total = ctx_count * exp_count * CAP
    in_rows = arrived_in.reshape(row_total, part_width)
    cot_rows = arrived_cot.reshape(row_total, part_width)
    up_part = up_weight[0]
    down_part = down_weight[0]
    contract_rows = (((0,), (0,)), ((), ()))
    contract_cols = (((1,), (1,)), ((), ()))

    def sum_all(term_rows):
        return lax.psum(term_rows.astype(jnp.bfloat16), "ctx").astype(jnp.float32)

    pre_full = sum_all(jnp.dot(in_rows, up_part, preferred_element_type=jnp.float32))
    activated = jax.nn.silu(pre_full).astype(jnp.bfloat16)
    grad_full = sum_all(
        lax.dot_general(cot_rows, down_part, contract_cols, preferred_element_type=jnp.float32)
    )
    pre_grad = (grad_full * silu_grad(pre_full)).astype(jnp.bfloat16)
    slot_out = jnp.dot(activated, down_part, preferred_element_type=jnp.float32).astype(
        jnp.bfloat16
    )
    down_grad = lax.dot_general(
        activated, cot_rows, contract_rows, preferred_element_type=jnp.float32
    ).astype(jnp.bfloat16)
    up_grad = lax.dot_general(
        in_rows, pre_grad, contract_rows, preferred_element_type=jnp.float32
    ).astype(jnp.bfloat16)
    slot_in_grad = lax.dot_general(
        pre_grad, up_part, contract_cols, preferred_element_type=jnp.float32
    ).astype(jnp.bfloat16)
    returned_out, returned_grad = (
        joined_exchange(
            slot_out.reshape(ctx_count, exp_count, CAP, part_width),
            ("ctx", "exp"),
            ("ctx", "exp"),
            (0, 1),
            (3, 1),
        ),
        joined_exchange(
            slot_in_grad.reshape(ctx_count, exp_count, CAP, part_width),
            ("ctx", "exp"),
            ("ctx", "exp"),
            (0, 1),
            (3, 1),
        ),
    )
    flat_out = returned_out.reshape(exp_count * CAP, model_width).astype(jnp.float32)
    flat_grad = returned_grad.reshape(exp_count * CAP, model_width).astype(jnp.float32)
    gathered_out = lax.dot_general(
        weigher,
        flat_out,
        contract_rows,
        precision=lax.Precision.HIGHEST,
        preferred_element_type=jnp.float32,
    )
    gathered_grad = lax.dot_general(
        picker,
        flat_grad,
        contract_rows,
        precision=lax.Precision.HIGHEST,
        preferred_element_type=jnp.float32,
    )
    layer_out = (hidden_in.astype(jnp.float32) + gathered_out).astype(jnp.bfloat16)
    input_grad = (cotangent[0].astype(jnp.float32) + gathered_grad).astype(jnp.bfloat16)
    return (layer_out[None], input_grad[None], up_grad[None], down_grad[None])


def solution(mesh):
    placed = (
        P("exp", "ctx", None),
        P("exp", "ctx", None),
        P("exp", "ctx", None),
        P("ctx", None),
        P("exp", "ctx", None),
        P("exp", None, "ctx"),
        P("exp", "ctx", None),
        P("exp", "ctx", None),
        P("exp", "ctx", None),
        P("exp", None),
    )
    return jax.shard_map(
        shards,
        mesh=mesh,
        in_specs=placed,
        out_specs=(
            P("exp", "ctx", None),
            P("exp", "ctx", None),
            P("exp", "ctx", None),
            P("exp", None, "ctx"),
        ),
        check_vma=False,
    )
```

profile of v0, /device:TPU:1, one launch (start us, length us, event | category | flops | bytes accessed | tf_op | source)
XLA Modules:
  0.0 664.1 jit_solution(6608124247840334252)
XLA Ops:
  9.3 4.5 reduce-window.6
  16.4 2.3 reshape_reshape.14
  19.3 1.8 copy.110
  21.1 16.7 %all-to-all-start.2 = ((bf16[256,1,1,4,448]{4,3,2,1,0:T(4,128)(2,1)}), bf16[256,1,1,4,448]{4,3,2,1,0:T(4,128)(2,1)}, u32[]{:S(2)}, u32[]{:S(2)}) async-start(bf16[256,1,1,4,448]{4,3,2,1,0:T(4,128)(2,1)} %copy.110), calls=%async_computation.2 | async-start | bytes 2097152 | tf_op jit(solution)/shard_map/all_to_all | solution.py:37
  38.9 201.2 %while.22 = (s32[]{:T(128)}, bf16[128,512]{1,0:T(8,128)(2,1)S(1)}, f32[128,2]{0,1:T(2,128)S(1)}, f32[128,2]{0,1:T(2,128)S(1)}, f32[128,2,512]{2,0,1:T(8,128)S(1)...) while((s32[]{:T(128)}, bf16[128,512]{1,0:T(8,128)(2,1)S(1)}, ...), condition=%wide.region_7.8_spmd.clone, body=%wide.region_3.7_spmd.clone.sunk | while | flops 67740288 | bytes 2839315 | solution.py:133
  38.9 3.5 collective-permute-start
  42.7 2.6 collective-permute-done
  46.0 4.4 collective-permute-start
  50.6 2.6 collective-permute-done
  53.9 4.4 collective-permute-start
  58.6 4.3 collective-permute-done
  63.6 5.2 collective-permute-start
  69.0 2.9 collective-permute-done
  72.5 4.4 collective-permute-start
  77.2 1.7 collective-permute-done
  79.6 4.4 collective-permute-start
  84.3 1.7 collective-permute-done
  86.6 13.3 %collective-permute-start = (bf16[128,512]{1,0:T(8,128)(2,1)S(1)}, bf16[128,512]{1,0:T(8,128)(2,1)S(1)}, u32[]{:S(2)}, u32[]{:S(2)}) collective-permute-start(bf16[128,512]{1,0:T(8,128)(2,1)S(1)} %get-tuple-element.483), channel_id=1, source_target_pairs={{0,16},{16,32},{32,48},{48,64},{64,80},{80,96},{96,112},{112,128},... | collective-permute-start | bytes 393224 | tf_op jit(solution)/shard_map/while/body/eval_jaxpr/ppermute | solution.py:16
  100.2 1.7 collective-permute-done
  102.5 10.9 %collective-permute-start = (bf16[128,512]{1,0:T(8,128)(2,1)S(1)}, bf16[128,512]{1,0:T(8,128)(2,1)S(1)}, u32[]{:S(2)}, u32[]{:S(2)}) collective-permute-start(bf16[128,512]{1,0:T(8,128)(2,1)S(1)} %get-tuple-element.483), channel_id=1, source_target_pairs={{0,16},{16,32},{32,48},{48,64},{64,80},{80,96},{96,112},{112,128},... | collective-permute-start | bytes 393224 | tf_op jit(solution)/shard_map/while/body/eval_jaxpr/ppermute | solution.py:16
  113.7 1.7 collective-permute-done
  116.1 12.3 %collective-permute-start = (bf16[128,512]{1,0:T(8,128)(2,1)S(1)}, bf16[128,512]{1,0:T(8,128)(2,1)S(1)}, u32[]{:S(2)}, u32[]{:S(2)}) collective-permute-start(bf16[128,512]{1,0:T(8,128)(2,1)S(1)} %get-tuple-element.483), channel_id=1, source_target_pairs={{0,16},{16,32},{32,48},{48,64},{64,80},{80,96},{96,112},{112,128},... | collective-permute-start | bytes 393224 | tf_op jit(solution)/shard_map/while/body/eval_jaxpr/ppermute | solution.py:16
  128.7 2.1 collective-permute-done
  131.4 16.8 %collective-permute-start = (bf16[128,512]{1,0:T(8,128)(2,1)S(1)}, bf16[128,512]{1,0:T(8,128)(2,1)S(1)}, u32[]{:S(2)}, u32[]{:S(2)}) collective-permute-start(bf16[128,512]{1,0:T(8,128)(2,1)S(1)} %get-tuple-element.483), channel_id=1, source_target_pairs={{0,16},{16,32},{32,48},{48,64},{64,80},{80,96},{96,112},{112,128},... | collective-permute-start | bytes 393224 | tf_op jit(solution)/shard_map/while/body/eval_jaxpr/ppermute | solution.py:16
  148.4 1.7 collective-permute-done
  150.8 18.1 %collective-permute-start = (bf16[128,512]{1,0:T(8,128)(2,1)S(1)}, bf16[128,512]{1,0:T(8,128)(2,1)S(1)}, u32[]{:S(2)}, u32[]{:S(2)}) collective-permute-start(bf16[128,512]{1,0:T(8,128)(2,1)S(1)} %get-tuple-element.483), channel_id=1, source_target_pairs={{0,16},{16,32},{32,48},{48,64},{64,80},{80,96},{96,112},{112,128},... | collective-permute-start | bytes 393224 | tf_op jit(solution)/shard_map/while/body/eval_jaxpr/ppermute | solution.py:16
  169.2 1.7 collective-permute-done
  171.6 29.1 %collective-permute-start = (bf16[128,512]{1,0:T(8,128)(2,1)S(1)}, bf16[128,512]{1,0:T(8,128)(2,1)S(1)}, u32[]{:S(2)}, u32[]{:S(2)}) collective-permute-start(bf16[128,512]{1,0:T(8,128)(2,1)S(1)} %get-tuple-element.483), channel_id=1, source_target_pairs={{0,16},{16,32},{32,48},{48,64},{64,80},{80,96},{96,112},{112,128},... | collective-permute-start | bytes 393224 | tf_op jit(solution)/shard_map/while/body/eval_jaxpr/ppermute | solution.py:16
  201.0 1.7 collective-permute-done
  203.3 8.0 %collective-permute-start = (bf16[128,512]{1,0:T(8,128)(2,1)S(1)}, bf16[128,512]{1,0:T(8,128)(2,1)S(1)}, u32[]{:S(2)}, u32[]{:S(2)}) collective-permute-start(bf16[128,512]{1,0:T(8,128)(2,1)S(1)} %get-tuple-element.483), channel_id=1, source_target_pairs={{0,16},{16,32},{32,48},{48,64},{64,80},{80,96},{96,112},{112,128},... | collective-permute-start | bytes 393224 | tf_op jit(solution)/shard_map/while/body/eval_jaxpr/ppermute | solution.py:16
  211.6 1.7 collective-permute-done
  214.0 10.5 %collective-permute-start = (bf16[128,512]{1,0:T(8,128)(2,1)S(1)}, bf16[128,512]{1,0:T(8,128)(2,1)S(1)}, u32[]{:S(2)}, u32[]{:S(2)}) collective-permute-start(bf16[128,512]{1,0:T(8,128)(2,1)S(1)} %get-tuple-element.483), channel_id=1, source_target_pairs={{0,16},{16,32},{32,48},{48,64},{64,80},{80,96},{96,112},{112,128},... | collective-permute-start | bytes 393224 | tf_op jit(solution)/shard_map/while/body/eval_jaxpr/ppermute | solution.py:16
  224.7 1.7 collective-permute-done
  227.1 10.4 %collective-permute-start = (bf16[128,512]{1,0:T(8,128)(2,1)S(1)}, bf16[128,512]{1,0:T(8,128)(2,1)S(1)}, u32[]{:S(2)}, u32[]{:S(2)}) collective-permute-start(bf16[128,512]{1,0:T(8,128)(2,1)S(1)} %get-tuple-element.483), channel_id=1, source_target_pairs={{0,16},{16,32},{32,48},{48,64},{64,80},{80,96},{96,112},{112,128},... | collective-permute-start | bytes 393224 | tf_op jit(solution)/shard_map/while/body/eval_jaxpr/ppermute | solution.py:16
  240.4 8.3 %fusion.16 = bf16[128,7168]{1,0:T(8,128)(2,1)S(1)} fusion(bf16[128,1024]{0,1:T(8,128)(2,1)S(1)} %bitcast.139, bf16[1024,7168]{1,0:T(8,128)(2,1)} %all-gather.2.cloned.1.call-done, bf16[1,128,7168]{2,1,0:T(8,128)(2,1)} %param.12), kind=kOutput, calls=%fused_computation.29 | convolution fusion | flops 1881800704 | bytes 18612224 | tf_op jit(solution)/shard_map/dot_general | solution.py:141
  249.9 3.1 reshape_reshape.12
  253.0 1.8 copy.104
  254.8 1.8 copy.105
  256.6 69.9 %all-to-all-start = ((bf16[256,1,1,4,448]{4,3,2,1,0:T(4,128)(2,1)}), bf16[256,1,1,4,448]{4,3,2,1,0:T(4,128)(2,1)}, u32[]{:S(2)}, u32[]{:S(2)}) async-start(bf16[256,1,1,4,448]{4,3,2,1,0:T(4,128)(2,1)} %copy.105), calls=%async_computation | async-start | bytes 2097152 | tf_op jit(solution)/shard_map/all_to_all | solution.py:37
  326.8 2.4 reshape_reshape.15
  329.2 4.0 convolution_convert_fusion.1
  333.3 24.4 %all-to-all-done = bf16[256,1,1,4,448]{4,3,2,1,0:T(4,128)(2,1)} async-done(((bf16[256,1,1,4,448]{4,3,2,1,0:T(4,128)(2,1)}), bf16[256,1,1,4,448]{4,3,2,1,0:T(4,128)(2,1)}, u32[]{:S(2)}, u32[]{:S(2)}) %all-to-all-start) | async-done | bytes 917536 | tf_op jit(solution)/shard_map/all_to_all | solution.py:37
  357.7 2.4 reshape_reshape.13
  360.1 3.8 convolution_convert_fusion.2
  363.9 187.7 %all-reduce.3.cloned.1.call-done = (bf16[1024,1024]{1,0:T(8,128)(2,1)}, bf16[1024,1024]{1,0:T(8,128)(2,1)}) async-done(((bf16[1024,1024]{1,0:T(8,128)(2,1)}, bf16[1024,1024]{1,0:T(8,128)(2,1)}), (bf16[1024,1024]{1,0:T(8,128)(2,1)}, bf16[1024,1024]{1,0:T(8,128)(2,1)})) %all-reduce.3.cloned.1.call-update) | async-done | bytes 4194320 | tf_op jit(solution)/shard_map/psum | solution.py:172
  551.6 3.9 fusion.29
  556.8 2.1 convolution_convert_fusion.5
  558.9 2.3 copy.111
  561.1 2.2 reshape_transpose_transpose_reshape_reshape_reshape.7
  563.3 14.0 %all-to-all-start.3 = ((bf16[256,1,1,4,448]{4,3,2,1,0:T(4,128)(2,1)}), bf16[256,1,1,4,448]{4,3,2,1,0:T(4,128)(2,1)}, u32[]{:S(2)}, u32[]{:S(2)}) async-start(bf16[256,1,1,4,448]{4,3,2,1,0:T(4,128)(2,1)} %bitcast.131), calls=%async_computation.3 | async-start | bytes 2097152 | tf_op jit(solution)/shard_map/all_to_all | solution.py:37
  577.3 4.3 convolution_convert_fusion.6
  581.6 2.3 copy.106
  583.8 2.2 reshape_transpose_transpose_reshape_reshape_reshape.6
  586.0 22.4 %all-to-all-done.3 = bf16[256,1,1,4,448]{4,3,2,1,0:T(4,128)(2,1)} async-done(((bf16[256,1,1,4,448]{4,3,2,1,0:T(4,128)(2,1)}), bf16[256,1,1,4,448]{4,3,2,1,0:T(4,128)(2,1)}, u32[]{:S(2)}, u32[]{:S(2)}) %all-to-all-start.3) | async-done | bytes 917536 | tf_op jit(solution)/shard_map/all_to_all | solution.py:37
  608.4 7.7 %all-to-all-start.1 = ((bf16[256,1,1,4,448]{4,3,2,1,0:T(4,128)(2,1)}), bf16[256,1,1,4,448]{4,3,2,1,0:T(4,128)(2,1)}, u32[]{:S(2)}, u32[]{:S(2)}) async-start(bf16[256,1,1,4,448]{4,3,2,1,0:T(4,128)(2,1)} %bitcast.130), calls=%async_computation.1 | async-start | bytes 2097152 | tf_op jit(solution)/shard_map/all_to_all | solution.py:37
  616.2 4.1 fusion.31
  620.3 2.5 fusion.32
  622.8 2.8 copy.121
  625.6 2.9 reshape_reshape_transpose_reshape.7
  628.5 4.7 fusion.19
  633.3 14.2 %all-to-all-done.1 = bf16[256,1,1,4,448]{4,3,2,1,0:T(4,128)(2,1)} async-done(((bf16[256,1,1,4,448]{4,3,2,1,0:T(4,128)(2,1)}), bf16[256,1,1,4,448]{4,3,2,1,0:T(4,128)(2,1)}, u32[]{:S(2)}, u32[]{:S(2)}) %all-to-all-start.1) | async-done | bytes 917536 | tf_op jit(solution)/shard_map/all_to_all | solution.py:37
  647.4 2.8 copy.122
  650.2 2.9 reshape_reshape_transpose_reshape.6
  653.1 4.1 fusion.20
  (221 shorter events, 23.7 us)
Async XLA Ops:
  7.2 352.9 %copy-start = (bf16[1,448,1024]{2,1,0:T(8,128)(2,1)S(1)}, bf16[1,448,1024]{2,1,0:T(8,128)(2,1)}, u32[]{:S(2)}) copy-start(bf16[1,448,1024]{2,1,0:T(8,128)(2,1)} %param.16) | copy-start | bytes 2752516
  7.2 7.8 %copy-start.2 = (bf16[1,128,7168]{2,1,0:T(8,128)(2,1)S(1)}, bf16[1,128,7168]{2,1,0:T(8,128)(2,1)}, u32[]{:S(2)}) copy-start(bf16[1,128,7168]{2,1,0:T(8,128)(2,1)} %param.18) | copy-start | bytes 5505028
  7.2 7.2 %copy-start.6 = (s32[1,128,8]{1,2,0:T(8,128)S(1)}, s32[1,128,8]{1,2,0:T(8,128)}, u32[]{:S(2)}) copy-start(s32[1,128,8]{1,2,0:T(8,128)} %param.19) | copy-start | bytes 12292
  7.2 7.3 %copy-start.7 = (f32[1,128,8]{1,2,0:T(8,128)S(1)}, f32[1,128,8]{1,2,0:T(8,128)}, u32[]{:S(2)}) copy-start(f32[1,128,8]{1,2,0:T(8,128)} %param.20) | copy-start | bytes 12292
  7.2 233.1 %all-gather.2.cloned.1.call-start = ((), (), s32[]{:S(2)}) async-start(), calls=%async_computation.4 | async-start | bytes 15597568 | tf_op jit(solution)/shard_map/all_gather | solution.py:143
  19.3 18.5 %copy-start.5 = (bf16[1,128,1024]{2,1,0:T(8,128)(2,1)S(1)}, bf16[1,128,1024]{2,1,0:T(8,128)(2,1)}, u32[]{:S(2)}) copy-start(bf16[1,128,1024]{2,1,0:T(8,128)(2,1)} %param.13) | copy-start | bytes 786436
  21.1 17.0 %copy-start.8 = (s32[1,16]{1,0:T(1,128)S(1)}, s32[1,16]{1,0:T(1,128)}, u32[]{:S(2)}) copy-start(s32[1,16]{1,0:T(1,128)} %param.21) | copy-start | bytes 196
  21.1 235.5 %all-to-all-start.2 = ((bf16[256,1,1,4,448]{4,3,2,1,0:T(4,128)(2,1)}), bf16[256,1,1,4,448]{4,3,2,1,0:T(4,128)(2,1)}, u32[]{:S(2)}, u32[]{:S(2)}) async-start(bf16[256,1,1,4,448]{4,3,2,1,0:T(4,128)(2,1)} %copy.110), calls=%async_computation.2 | async-start | bytes 2097152 | tf_op jit(solution)/shard_map/all_to_all | solution.py:37
  38.9 6.4 collective-permute-start
  46.0 7.3 %collective-permute-start = (bf16[128,512]{1,0:T(8,128)(2,1)S(1)}, bf16[128,512]{1,0:T(8,128)(2,1)S(1)}, u32[]{:S(2)}, u32[]{:S(2)}) collective-permute-start(bf16[128,512]{1,0:T(8,128)(2,1)S(1)} %get-tuple-element.483), channel_id=1, source_target_pairs={{0,16},{16,32},{32,48},{48,64},{64,80},{80,96},{96,112},{112,128},... | collective-permute-start | bytes 393224 | tf_op jit(solution)/shard_map/while/body/eval_jaxpr/ppermute | solution.py:16
  53.9 9.0 %collective-permute-start = (bf16[128,512]{1,0:T(8,128)(2,1)S(1)}, bf16[128,512]{1,0:T(8,128)(2,1)S(1)}, u32[]{:S(2)}, u32[]{:S(2)}) collective-permute-start(bf16[128,512]{1,0:T(8,128)(2,1)S(1)} %get-tuple-element.483), channel_id=1, source_target_pairs={{0,16},{16,32},{32,48},{48,64},{64,80},{80,96},{96,112},{112,128},... | collective-permute-start | bytes 393224 | tf_op jit(solution)/shard_map/while/body/eval_jaxpr/ppermute | solution.py:16
  63.6 8.3 %collective-permute-start = (bf16[128,512]{1,0:T(8,128)(2,1)S(1)}, bf16[128,512]{1,0:T(8,128)(2,1)S(1)}, u32[]{:S(2)}, u32[]{:S(2)}) collective-permute-start(bf16[128,512]{1,0:T(8,128)(2,1)S(1)} %get-tuple-element.483), channel_id=1, source_target_pairs={{0,16},{16,32},{32,48},{48,64},{64,80},{80,96},{96,112},{112,128},... | collective-permute-start | bytes 393224 | tf_op jit(solution)/shard_map/while/body/eval_jaxpr/ppermute | solution.py:16
  72.5 6.4 collective-permute-start
  79.6 6.3 collective-permute-start
  86.6 15.2 %collective-permute-start = (bf16[128,512]{1,0:T(8,128)(2,1)S(1)}, bf16[128,512]{1,0:T(8,128)(2,1)S(1)}, u32[]{:S(2)}, u32[]{:S(2)}) collective-permute-start(bf16[128,512]{1,0:T(8,128)(2,1)S(1)} %get-tuple-element.483), channel_id=1, source_target_pairs={{0,16},{16,32},{32,48},{48,64},{64,80},{80,96},{96,112},{112,128},... | collective-permute-start | bytes 393224 | tf_op jit(solution)/shard_map/while/body/eval_jaxpr/ppermute | solution.py:16
  102.5 12.9 %collective-permute-start = (bf16[128,512]{1,0:T(8,128)(2,1)S(1)}, bf16[128,512]{1,0:T(8,128)(2,1)S(1)}, u32[]{:S(2)}, u32[]{:S(2)}) collective-permute-start(bf16[128,512]{1,0:T(8,128)(2,1)S(1)} %get-tuple-element.483), channel_id=1, source_target_pairs={{0,16},{16,32},{32,48},{48,64},{64,80},{80,96},{96,112},{112,128},... | collective-permute-start | bytes 393224 | tf_op jit(solution)/shard_map/while/body/eval_jaxpr/ppermute | solution.py:16
  116.1 14.7 %collective-permute-start = (bf16[128,512]{1,0:T(8,128)(2,1)S(1)}, bf16[128,512]{1,0:T(8,128)(2,1)S(1)}, u32[]{:S(2)}, u32[]{:S(2)}) collective-permute-start(bf16[128,512]{1,0:T(8,128)(2,1)S(1)} %get-tuple-element.483), channel_id=1, source_target_pairs={{0,16},{16,32},{32,48},{48,64},{64,80},{80,96},{96,112},{112,128},... | collective-permute-start | bytes 393224 | tf_op jit(solution)/shard_map/while/body/eval_jaxpr/ppermute | solution.py:16
  131.4 18.7 %collective-permute-start = (bf16[128,512]{1,0:T(8,128)(2,1)S(1)}, bf16[128,512]{1,0:T(8,128)(2,1)S(1)}, u32[]{:S(2)}, u32[]{:S(2)}) collective-permute-start(bf16[128,512]{1,0:T(8,128)(2,1)S(1)} %get-tuple-element.483), channel_id=1, source_target_pairs={{0,16},{16,32},{32,48},{48,64},{64,80},{80,96},{96,112},{112,128},... | collective-permute-start | bytes 393224 | tf_op jit(solution)/shard_map/while/body/eval_jaxpr/ppermute | solution.py:16
  150.8 20.1 %collective-permute-start = (bf16[128,512]{1,0:T(8,128)(2,1)S(1)}, bf16[128,512]{1,0:T(8,128)(2,1)S(1)}, u32[]{:S(2)}, u32[]{:S(2)}) collective-permute-start(bf16[128,512]{1,0:T(8,128)(2,1)S(1)} %get-tuple-element.483), channel_id=1, source_target_pairs={{0,16},{16,32},{32,48},{48,64},{64,80},{80,96},{96,112},{112,128},... | collective-permute-start | bytes 393224 | tf_op jit(solution)/shard_map/while/body/eval_jaxpr/ppermute | solution.py:16
  171.6 31.1 %collective-permute-start = (bf16[128,512]{1,0:T(8,128)(2,1)S(1)}, bf16[128,512]{1,0:T(8,128)(2,1)S(1)}, u32[]{:S(2)}, u32[]{:S(2)}) collective-permute-start(bf16[128,512]{1,0:T(8,128)(2,1)S(1)} %get-tuple-element.483), channel_id=1, source_target_pairs={{0,16},{16,32},{32,48},{48,64},{64,80},{80,96},{96,112},{112,128},... | collective-permute-start | bytes 393224 | tf_op jit(solution)/shard_map/while/body/eval_jaxpr/ppermute | solution.py:16
  203.3 10.0 %collective-permute-start = (bf16[128,512]{1,0:T(8,128)(2,1)S(1)}, bf16[128,512]{1,0:T(8,128)(2,1)S(1)}, u32[]{:S(2)}, u32[]{:S(2)}) collective-permute-start(bf16[128,512]{1,0:T(8,128)(2,1)S(1)} %get-tuple-element.483), channel_id=1, source_target_pairs={{0,16},{16,32},{32,48},{48,64},{64,80},{80,96},{96,112},{112,128},... | collective-permute-start | bytes 393224 | tf_op jit(solution)/shard_map/while/body/eval_jaxpr/ppermute | solution.py:16
  214.0 12.4 %collective-permute-start = (bf16[128,512]{1,0:T(8,128)(2,1)S(1)}, bf16[128,512]{1,0:T(8,128)(2,1)S(1)}, u32[]{:S(2)}, u32[]{:S(2)}) collective-permute-start(bf16[128,512]{1,0:T(8,128)(2,1)S(1)} %get-tuple-element.483), channel_id=1, source_target_pairs={{0,16},{16,32},{32,48},{48,64},{64,80},{80,96},{96,112},{112,128},... | collective-permute-start | bytes 393224 | tf_op jit(solution)/shard_map/while/body/eval_jaxpr/ppermute | solution.py:16
  227.1 12.3 %collective-permute-start = (bf16[128,512]{1,0:T(8,128)(2,1)S(1)}, bf16[128,512]{1,0:T(8,128)(2,1)S(1)}, u32[]{:S(2)}, u32[]{:S(2)}) collective-permute-start(bf16[128,512]{1,0:T(8,128)(2,1)S(1)} %get-tuple-element.483), channel_id=1, source_target_pairs={{0,16},{16,32},{32,48},{48,64},{64,80},{80,96},{96,112},{112,128},... | collective-permute-start | bytes 393224 | tf_op jit(solution)/shard_map/while/body/eval_jaxpr/ppermute | solution.py:16
  256.6 101.1 %all-to-all-start = ((bf16[256,1,1,4,448]{4,3,2,1,0:T(4,128)(2,1)}), bf16[256,1,1,4,448]{4,3,2,1,0:T(4,128)(2,1)}, u32[]{:S(2)}, u32[]{:S(2)}) async-start(bf16[256,1,1,4,448]{4,3,2,1,0:T(4,128)(2,1)} %copy.105), calls=%async_computation | async-start | bytes 2097152 | tf_op jit(solution)/shard_map/all_to_all | solution.py:37
  326.6 225.0 %all-reduce.3.cloned.1.call-start = ((), (), s32[]{:S(2)}) async-start(), calls=%async_computation.5 | async-start | bytes 8388608 | tf_op jit(solution)/shard_map/psum | solution.py:172
  555.5 1.3 copy-start.1
  563.3 45.1 %all-to-all-start.3 = ((bf16[256,1,1,4,448]{4,3,2,1,0:T(4,128)(2,1)}), bf16[256,1,1,4,448]{4,3,2,1,0:T(4,128)(2,1)}, u32[]{:S(2)}, u32[]{:S(2)}) async-start(bf16[256,1,1,4,448]{4,3,2,1,0:T(4,128)(2,1)} %bitcast.131), calls=%async_computation.3 | async-start | bytes 2097152 | tf_op jit(solution)/shard_map/all_to_all | solution.py:37
  608.4 39.0 %all-to-all-start.1 = ((bf16[256,1,1,4,448]{4,3,2,1,0:T(4,128)(2,1)}), bf16[256,1,1,4,448]{4,3,2,1,0:T(4,128)(2,1)}, u32[]{:S(2)}, u32[]{:S(2)}) async-start(bf16[256,1,1,4,448]{4,3,2,1,0:T(4,128)(2,1)} %bitcast.130), calls=%async_computation.1 | async-start | bytes 2097152 | tf_op jit(solution)/shard_map/all_to_all | solution.py:37
  616.2 4.1 copy-start.3
  616.2 4.1 copy-start.4
Sparse Core Ops, SparseCore 0:
  10.7 179.2 all-gather.1
  364.0 187.4 all-reduce.2
where the time goes:
time: 665 us; the launch traced here: 664 us
  waiting for transfers between devices  280 us (42%)
  starting transfers between devices  264 us (40%)
  matrix products  49.4 us (7%)
  local copies, waits for them, and re-layouts  40.9 us (6%)
  between operations  14.3 us (2%)
  other arithmetic  13.6 us (2%)
    psum x1, waiting for transfers between devices, sum_all(): return lax.psum(term_rows.astype(jnp.bfloat16), 'ctx').astype(jnp.float32)  188 us
    ppermute x15, starting transfers between devices, shifted(): return lax.ppermute(shard, axis, pairs)  156 us
    all_to_all x4, starting transfers between devices, joined_exchange(): lax.all_to_all(pieces, axis, split_axis=0, concat_axis=0, tiled=True)  108 us
    all_to_all x4, waiting for transfers between devices, joined_exchange(): lax.all_to_all(pieces, axis, split_axis=0, concat_axis=0, tiled=True)  61 us
    ppermute x15, waiting for transfers between devices, shifted(): return lax.ppermute(shard, axis, pairs)  31.3 us
  transfers between devices with their start and end apart: 21, of which 19 were waited for; matrix products, arithmetic and copies ran while one was open for 11% of the time, Pallas kernels for 0%

commit v1 on v0

--- a/solution.py
+++ b/solution.py
@@ -1,3 +1,4 @@
+import functools
 import math
 import jax
 import jax.numpy as jnp
@@ -8,6 +9,14 @@
 HEADS = 2
 CAP = 4
 BLOCK = 128
+
+
+def reach_sector(local_block, bus_axis):
+    aux = jax.lax.all_gather(local_block, bus_axis).sum(axis=0)
+    return aux
+
+
+tails_edit = functools.partial(reach_sector, bus_axis="ctx")
 
 
 def shifted(shard, axis, by):
@@ -169,7 +178,7 @@
     contract_cols = (((1,), (1,)), ((), ()))
 
     def sum_all(term_rows):
-        return lax.psum(term_rows.astype(jnp.bfloat16), "ctx").astype(jnp.float32)
+        return tails_edit(term_rows.astype(jnp.bfloat16)).astype(jnp.float32)
 
     pre_full = sum_all(jnp.dot(in_rows, up_part, preferred_element_type=jnp.float32))
     activated = jax.nn.silu(pre_full).astype(jnp.bfloat16)

time: 665 us -> 1070 us (1.61)
  waiting for transfers between devices: 280 us -> 599 us
  blocking collectives: 0 us -> 173 us
  starting transfers between devices: 264 us -> 149 us
  other arithmetic: 13.6 us -> 41.2 us
    all_gather x0 -> x2, waiting for transfers between devices: none -> 545 us  [reach_sector(): aux = jax.lax.all_gather(local_block, bus_axis).sum(axis=0)]
    psum x1 -> x0, waiting for transfers between devices: 188 us -> none  [sum_all(): return lax.psum(term_rows.astype(jnp.bfloat16), 'ctx').astype(jnp.float32)]
    all_to_all x0 -> x2, blocking collectives: none -> 173 us  [joined_exchange(): lax.all_to_all(pieces, axis, split_axis=0, concat_axis=0, tiled=True)]
    all_to_all x4 -> x2, starting transfers between devices: 108 us -> 13.9 us  [joined_exchange(): lax.all_to_all(pieces, axis, split_axis=0, concat_axis=0, tiled=True)]
    all_to_all x4 -> x2, waiting for transfers between devices: 61 us -> 18.8 us  [joined_exchange(): lax.all_to_all(pieces, axis, split_axis=0, concat_axis=0, tiled=True)]
    reduce_sum x0 -> x2, other arithmetic: none -> 27.5 us  [reach_sector(): aux = jax.lax.all_gather(local_block, bus_axis).sum(axis=0)]
    ppermute x15, starting transfers between devices: 156 us -> 135 us  [shifted(): return lax.ppermute(shard, axis, pairs)]
  transfers between devices with their start and end apart: 21 -> 20, of which waited for: 19 -> 18; matrix products, arithmetic and copies ran while one was open for 11% -> 9% of each run, Pallas kernels for 0% -> 0%
where the time goes in v1:
time: 1070 us
  waiting for transfers between devices  599 us (56%)
  blocking collectives  173 us (16%)
  starting transfers between devices  149 us (14%)
  matrix products  48.4 us (5%)
  other arithmetic  41.2 us (4%)
  local copies, waits for them, and re-layouts  39.5 us (4%)
  between operations  14.1 us (1%)
    all_gather x2, waiting for transfers between devices, reach_sector(): aux = jax.lax.all_gather(local_block, bus_axis).sum(axis=0)  545 us
    all_to_all x2, blocking collectives, joined_exchange(): lax.all_to_all(pieces, axis, split_axis=0, concat_axis=0, tiled=True)  173 us
    ppermute x15, starting transfers between devices, shifted(): return lax.ppermute(shard, axis, pairs)  135 us
    ppermute x15, waiting for transfers between devices, shifted(): return lax.ppermute(shard, axis, pairs)  35 us
    reduce_sum x2, other arithmetic, reach_sector(): aux = jax.lax.all_gather(local_block, bus_axis).sum(axis=0)  27.5 us
  transfers between devices with their start and end apart: 20, of which 18 were waited for; matrix products, arithmetic and copies ran while one was open for 9% of the time, Pallas kernels for 0%

profile of v1, /device:TPU:1, one launch (start us, length us, event | category | flops | bytes accessed | tf_op | source)
XLA Modules:
  0.0 1065.5 jit_solution(6372221204017196223)
XLA Ops:
  9.3 4.5 reduce-window.6
  15.6 183.9 %while.22 = (s32[]{:T(128)}, bf16[128,512]{1,0:T(8,128)(2,1)S(1)}, f32[128,2]{0,1:T(2,128)S(1)}, f32[128,2]{0,1:T(2,128)S(1)}, f32[128,2,512]{2,0,1:T(8,128)S(1)...) while((s32[]{:T(128)}, bf16[128,512]{1,0:T(8,128)(2,1)S(1)}, ...), condition=%wide.region_7.8_spmd.clone, body=%wide.region_3.7_spmd.clone.sunk | while | flops 67740288 | bytes 2839315 | solution.py:142
  15.6 4.6 collective-permute-start
  20.4 1.7 collective-permute-done
  22.8 4.4 collective-permute-start
  27.4 3.1 collective-permute-done
  31.2 4.4 collective-permute-start
  35.8 1.7 collective-permute-done
  38.2 4.4 collective-permute-start
  42.8 2.3 collective-permute-done
  45.7 4.4 collective-permute-start
  50.3 1.7 collective-permute-done
  52.7 4.4 collective-permute-start
  57.3 3.9 collective-permute-done
  61.9 4.4 collective-permute-start
  66.6 1.7 collective-permute-done
  68.9 4.4 collective-permute-start
  73.5 4.6 collective-permute-done
  78.8 9.7 collective-permute-start
  88.7 1.7 collective-permute-done
  91.1 9.8 collective-permute-start
  101.1 1.7 collective-permute-done
  103.5 13.8 %collective-permute-start = (bf16[128,512]{1,0:T(8,128)(2,1)S(1)}, bf16[128,512]{1,0:T(8,128)(2,1)S(1)}, u32[]{:S(2)}, u32[]{:S(2)}) collective-permute-start(bf16[128,512]{1,0:T(8,128)(2,1)S(1)} %get-tuple-element.481), channel_id=1, source_target_pairs={{0,16},{16,32},{32,48},{48,64},{64,80},{80,96},{96,112},{112,128},... | collective-permute-start | bytes 393224 | tf_op jit(solution)/shard_map/while/body/eval_jaxpr/ppermute | solution.py:25
  117.5 1.7 collective-permute-done
  119.9 18.8 %collective-permute-start = (bf16[128,512]{1,0:T(8,128)(2,1)S(1)}, bf16[128,512]{1,0:T(8,128)(2,1)S(1)}, u32[]{:S(2)}, u32[]{:S(2)}) collective-permute-start(bf16[128,512]{1,0:T(8,128)(2,1)S(1)} %get-tuple-element.481), channel_id=1, source_target_pairs={{0,16},{16,32},{32,48},{48,64},{64,80},{80,96},{96,112},{112,128},... | collective-permute-start | bytes 393224 | tf_op jit(solution)/shard_map/while/body/eval_jaxpr/ppermute | solution.py:25
  138.9 1.7 collective-permute-done
  141.3 17.1 %collective-permute-start = (bf16[128,512]{1,0:T(8,128)(2,1)S(1)}, bf16[128,512]{1,0:T(8,128)(2,1)S(1)}, u32[]{:S(2)}, u32[]{:S(2)}) collective-permute-start(bf16[128,512]{1,0:T(8,128)(2,1)S(1)} %get-tuple-element.481), channel_id=1, source_target_pairs={{0,16},{16,32},{32,48},{48,64},{64,80},{80,96},{96,112},{112,128},... | collective-permute-start | bytes 393224 | tf_op jit(solution)/shard_map/while/body/eval_jaxpr/ppermute | solution.py:25
  158.7 4.3 collective-permute-done
  163.7 22.9 %collective-permute-start = (bf16[128,512]{1,0:T(8,128)(2,1)S(1)}, bf16[128,512]{1,0:T(8,128)(2,1)S(1)}, u32[]{:S(2)}, u32[]{:S(2)}) collective-permute-start(bf16[128,512]{1,0:T(8,128)(2,1)S(1)} %get-tuple-element.481), channel_id=1, source_target_pairs={{0,16},{16,32},{32,48},{48,64},{64,80},{80,96},{96,112},{112,128},... | collective-permute-start | bytes 393224 | tf_op jit(solution)/shard_map/while/body/eval_jaxpr/ppermute | solution.py:25
  186.8 1.7 collective-permute-done
  189.2 7.7 collective-permute-start
  197.1 1.7 collective-permute-done
  200.4 8.3 fusion.16
  210.0 3.1 reshape_reshape.12
  213.0 1.8 copy.104
  215.7 109.9 %all_to_all.20 = bf16[256,1,1,4,448]{4,3,2,1,0:T(4,128)(2,1)} all-to-all(bf16[256,1,1,4,448]{4,3,2,1,0:T(4,128)(2,1)S(1)} %copy.105), channel_id=1, replica_groups=mesh['ctx'=16,'exp'=16] {'ctx','exp'}, dimensions={0} | all-to-all | bytes 1835008 | tf_op jit(solution)/shard_map/all_to_all | solution.py:46
  325.6 2.4 reshape_reshape.13
  328.0 4.1 convolution_convert_fusion.2
  332.3 2.8 fusion.21
  335.1 3.1 reshape_reshape.14
  338.2 2.0 copy.109
  341.0 63.4 %all_to_all.21 = bf16[256,1,1,4,448]{4,3,2,1,0:T(4,128)(2,1)} all-to-all(bf16[256,1,1,4,448]{4,3,2,1,0:T(4,128)(2,1)S(1)} %copy.110), channel_id=1, replica_groups=mesh['ctx'=16,'exp'=16] {'ctx','exp'}, dimensions={0} | all-to-all | bytes 1835008 | tf_op jit(solution)/shard_map/all_to_all | solution.py:46
  404.4 2.4 reshape_reshape.15
  406.8 3.8 convolution_convert_fusion.1
  410.6 246.5 %all-gather.8.cloned.1.call-done = bf16[16384,1024]{1,0:T(8,128)(2,1)} async-done(((bf16[1024,1024]{1,0:T(8,128)(2,1)}), bf16[16384,1024]{1,0:T(8,128)(2,1)}) %all-gather.8.cloned.1.call-update) | async-done | bytes 33554448 | tf_op jit(solution)/shard_map/all_gather | solution.py:15
  657.1 14.4 %reduce_sum.119 = bf16[1024,1024]{1,0:T(8,128)(2,1)} reduce(bf16[16,1024,1024]{2,1,0:T(8,128)(2,1)} %bitcast.132, bf16[]{:T(256)} %constant.150.clone.1), dimensions={0}, to_apply=%region_13.14 | reduce | flops 15728640 | bytes 35651584 | tf_op jit(solution)/shard_map/reduce_sum | solution.py:15
  671.5 4.0 convolution_convert_fusion.6
  675.6 2.2 copy.106
  677.8 2.2 reshape_transpose_transpose_reshape_reshape_reshape.6
  680.0 6.8 all-to-all-start.1
  686.8 298.4 %all-gather.10.cloned.1.call-done = bf16[16384,1024]{1,0:T(8,128)(2,1)} async-done(((bf16[1024,1024]{1,0:T(8,128)(2,1)}), bf16[16384,1024]{1,0:T(8,128)(2,1)}) %all-gather.10.cloned.1.call-update) | async-done | bytes 33554448 | tf_op jit(solution)/shard_map/all_gather | solution.py:15
  985.2 13.1 %reduce_sum.121 = bf16[1024,1024]{1,0:T(8,128)(2,1)} reduce(bf16[16,1024,1024]{2,1,0:T(8,128)(2,1)} %bitcast.133, bf16[]{:T(256)} %constant.150.clone.1), dimensions={0}, to_apply=%region_15.16 | reduce | flops 15728640 | bytes 35651584 | tf_op jit(solution)/shard_map/reduce_sum | solution.py:15
  998.3 4.0 fusion.29
  1006.1 2.2 reshape_transpose_transpose_reshape_reshape_reshape.7
  1008.3 7.1 all-to-all-start.3
  1015.4 4.1 fusion.31
  1019.5 2.5 fusion.32
  1022.0 2.8 copy.122
  1024.8 2.9 reshape_reshape_transpose_reshape.6
  1027.7 18.8 %all-to-all-done.3 = bf16[256,1,1,4,448]{4,3,2,1,0:T(4,128)(2,1)} async-done(((bf16[256,1,1,4,448]{4,3,2,1,0:T(4,128)(2,1)}), bf16[256,1,1,4,448]{4,3,2,1,0:T(4,128)(2,1)}, u32[]{:S(2)}, u32[]{:S(2)}) %all-to-all-start.3) | async-done | bytes 917536 | tf_op jit(solution)/shard_map/all_to_all | solution.py:46
  1046.5 2.8 copy.121
  1049.3 2.2 reshape_reshape_transpose_reshape.7
  1051.5 4.5 fusion.19
  1056.0 3.0 fusion.20
  (228 shorter events, 24.2 us)
Async XLA Ops:
  7.2 399.6 %copy-start = (bf16[1,1024,448]{1,2,0:T(8,128)(2,1)S(1)}, bf16[1,1024,448]{1,2,0:T(8,128)(2,1)}, u32[]{:S(2)}) copy-start(bf16[1,1024,448]{1,2,0:T(8,128)(2,1)} %param.17) | copy-start | bytes 2752516
  7.2 7.2 copy-start.6
  7.2 7.6 copy-start.10
  7.2 193.2 %all-gather.6.cloned.1.call-start = ((), (), s32[]{:S(2)}) async-start(), calls=%async_computation.4 | async-start | bytes 15597568 | tf_op jit(solution)/shard_map/all_gather | solution.py:152
  8.3 648.9 %all-gather.8.cloned.1.call-start = ((), (), s32[]{:S(2)}) async-start(), calls=%async_computation.5 | async-start | bytes 35651584 | tf_op jit(solution)/shard_map/all_gather | solution.py:15
  15.5 184.1 %copy-start.7 = (s32[1,128,8]{1,2,0:T(8,128)S(1)}, s32[1,128,8]{1,2,0:T(8,128)}, u32[]{:S(2)}) copy-start(s32[1,128,8]{1,2,0:T(8,128)} %param.19) | copy-start | bytes 12292
  15.6 184.2 %copy-start.8 = (f32[1,128,8]{1,2,0:T(8,128)S(1)}, f32[1,128,8]{1,2,0:T(8,128)}, u32[]{:S(2)}) copy-start(f32[1,128,8]{1,2,0:T(8,128)} %param.20) | copy-start | bytes 12292
  15.6 6.5 collective-permute-start
  22.8 7.7 collective-permute-start
  31.2 6.3 collective-permute-start
  38.2 6.9 collective-permute-start
  45.7 6.3 collective-permute-start
  52.7 8.5 collective-permute-start
  61.9 6.3 collective-permute-start
  68.9 9.2 collective-permute-start
  78.8 11.6 %collective-permute-start = (bf16[128,512]{1,0:T(8,128)(2,1)S(1)}, bf16[128,512]{1,0:T(8,128)(2,1)S(1)}, u32[]{:S(2)}, u32[]{:S(2)}) collective-permute-start(bf16[128,512]{1,0:T(8,128)(2,1)S(1)} %get-tuple-element.481), channel_id=1, source_target_pairs={{0,16},{16,32},{32,48},{48,64},{64,80},{80,96},{96,112},{112,128},... | collective-permute-start | bytes 393224 | tf_op jit(solution)/shard_map/while/body/eval_jaxpr/ppermute | solution.py:25
  91.1 11.7 %collective-permute-start = (bf16[128,512]{1,0:T(8,128)(2,1)S(1)}, bf16[128,512]{1,0:T(8,128)(2,1)S(1)}, u32[]{:S(2)}, u32[]{:S(2)}) collective-permute-start(bf16[128,512]{1,0:T(8,128)(2,1)S(1)} %get-tuple-element.481), channel_id=1, source_target_pairs={{0,16},{16,32},{32,48},{48,64},{64,80},{80,96},{96,112},{112,128},... | collective-permute-start | bytes 393224 | tf_op jit(solution)/shard_map/while/body/eval_jaxpr/ppermute | solution.py:25
  103.5 15.7 %collective-permute-start = (bf16[128,512]{1,0:T(8,128)(2,1)S(1)}, bf16[128,512]{1,0:T(8,128)(2,1)S(1)}, u32[]{:S(2)}, u32[]{:S(2)}) collective-permute-start(bf16[128,512]{1,0:T(8,128)(2,1)S(1)} %get-tuple-element.481), channel_id=1, source_target_pairs={{0,16},{16,32},{32,48},{48,64},{64,80},{80,96},{96,112},{112,128},... | collective-permute-start | bytes 393224 | tf_op jit(solution)/shard_map/while/body/eval_jaxpr/ppermute | solution.py:25
  119.9 20.8 %collective-permute-start = (bf16[128,512]{1,0:T(8,128)(2,1)S(1)}, bf16[128,512]{1,0:T(8,128)(2,1)S(1)}, u32[]{:S(2)}, u32[]{:S(2)}) collective-permute-start(bf16[128,512]{1,0:T(8,128)(2,1)S(1)} %get-tuple-element.481), channel_id=1, source_target_pairs={{0,16},{16,32},{32,48},{48,64},{64,80},{80,96},{96,112},{112,128},... | collective-permute-start | bytes 393224 | tf_op jit(solution)/shard_map/while/body/eval_jaxpr/ppermute | solution.py:25
  141.3 21.6 %collective-permute-start = (bf16[128,512]{1,0:T(8,128)(2,1)S(1)}, bf16[128,512]{1,0:T(8,128)(2,1)S(1)}, u32[]{:S(2)}, u32[]{:S(2)}) collective-permute-start(bf16[128,512]{1,0:T(8,128)(2,1)S(1)} %get-tuple-element.481), channel_id=1, source_target_pairs={{0,16},{16,32},{32,48},{48,64},{64,80},{80,96},{96,112},{112,128},... | collective-permute-start | bytes 393224 | tf_op jit(solution)/shard_map/while/body/eval_jaxpr/ppermute | solution.py:25
  163.7 24.9 %collective-permute-start = (bf16[128,512]{1,0:T(8,128)(2,1)S(1)}, bf16[128,512]{1,0:T(8,128)(2,1)S(1)}, u32[]{:S(2)}, u32[]{:S(2)}) collective-permute-start(bf16[128,512]{1,0:T(8,128)(2,1)S(1)} %get-tuple-element.481), channel_id=1, source_target_pairs={{0,16},{16,32},{32,48},{48,64},{64,80},{80,96},{96,112},{112,128},... | collective-permute-start | bytes 393224 | tf_op jit(solution)/shard_map/while/body/eval_jaxpr/ppermute | solution.py:25
  189.2 9.6 collective-permute-start
  332.1 653.1 %all-gather.10.cloned.1.call-start = ((), (), s32[]{:S(2)}) async-start(), calls=%async_computation.6 | async-start | bytes 35651584 | tf_op jit(solution)/shard_map/all_gather | solution.py:15
  680.0 328.3 %all-to-all-start.1 = ((bf16[256,1,1,4,448]{4,3,2,1,0:T(4,128)(2,1)}), bf16[256,1,1,4,448]{4,3,2,1,0:T(4,128)(2,1)}, u32[]{:S(2)}, u32[]{:S(2)}) async-start(bf16[256,1,1,4,448]{4,3,2,1,0:T(4,128)(2,1)} %bitcast.135), calls=%async_computation.1 | async-start | bytes 2097152 | tf_op jit(solution)/shard_map/all_to_all | solution.py:46
  998.3 5.4 copy-start.9
  1002.3 1.4 copy-start.3
  1008.3 38.2 %all-to-all-start.3 = ((bf16[256,1,1,4,448]{4,3,2,1,0:T(4,128)(2,1)}), bf16[256,1,1,4,448]{4,3,2,1,0:T(4,128)(2,1)}, u32[]{:S(2)}, u32[]{:S(2)}) async-start(bf16[256,1,1,4,448]{4,3,2,1,0:T(4,128)(2,1)} %bitcast.134), calls=%async_computation.3 | async-start | bytes 2097152 | tf_op jit(solution)/shard_map/all_to_all | solution.py:46
  1015.4 4.1 copy-start.2
  1015.4 4.1 copy-start.5
  1051.5 4.6 copy-start.4
  1056.0 3.0 copy-start.1
Sparse Core Ops, SparseCore 0:
  10.7 162.8 all-gather.5
  332.2 324.9 all-gather.7
  659.9 325.2 all-gather.9
